TPU v7x, 256 devices: a whole 4x4x8 slice. The times are simulated.
256 devices in a mesh: seq: 32 (over z, x), head: 8 (over y, core).
Axes of the slice: x: 4, y: 4, z: 8, core: 2. Of those that a mesh axis runs over, the one named last changes fastest.
Arguments:
- queries: bfloat16 [32768, 4096], P('seq', 'head'), may hold values from -6 to 6
- key_rows: bfloat16 [32768, 4096], P('seq', 'head'), may hold values from -6 to 6
- value_rows: bfloat16 [32768, 4096], P('seq', 'head'), may hold values from -6 to 6
- out_grad: bfloat16 [32768, 4096], P('seq', 'head'), may hold values from -6 to 6
- cache_states: bfloat16 [32, 32, 128, 128], P('seq', 'head'), may hold values from -96 to 96
- session_start: int32 [32], P('seq'), may hold values from 0 to 1024, as said below
- cache_owner: int32 [32], replicated, may hold values from 0 to 31, as said below
- probe_gate: float32 [32768], P('seq'), may hold values from 0.1 to 4.5
- steer_vector: bfloat16 [32, 128], P('head'), may hold values from -0.09375 to 0.09375
Outputs:
- grad_queries: bfloat16 [32768, 4096], P('seq', 'head')
- grad_keys: bfloat16 [32768, 4096], P('seq', 'head')
- grad_values: bfloat16 [32768, 4096], P('seq', 'head')
- grad_cache: bfloat16 [32, 32, 128, 128], P('seq', 'head')
- grad_steer: float32 [32, 128], P('head')
- grad_gate: float32 [32768], P('seq')
Inputs may be any that keep to these rules, and one draw needn't show every extreme that they name: session_start[b] is the position of the session beginning in block b, or 1024 where none does; it is 512 for every b with b % 4 == 3, so no session reaches across more than 5 blocks. `cache_owner`: a permutation of the slots.
All inputs are finite; a program needn't handle non-finite values.
Results may differ from a plain program's by a relative error of at most 0.007.
Values may be sent and summed in bfloat16 or wider, within the bound.
No kernel may reach another device: no remote copies, remote signals or barrier semaphores. Data moves between devices by JAX's collectives and lax.ppermute only.
A program may use at most 128 MiB of HBM per device.

v0:
```python
import math
import jax
import jax.numpy as jnp
from jax import lax
from jax.sharding import PartitionSpec as P

DK = 128
DV = 128


def prefix(part, axis, combine, identity, reverse):
    count = lax.axis_size(axis)
    place = lax.axis_index(axis)
    ahead = count - 1 - place if reverse else place
    gathered = jax.tree.map(lambda a: lax.all_gather(a, axis), part)
    state = jax.tree.map(lambda a, e: jnp.zeros_like(a) + jnp.asarray(e, a.dtype), part, identity)

    def one(turn, state):
        source = count - 1 - turn if reverse else turn
        return combine(
            state, jax.tree.map(lambda a: lax.dynamic_index_in_dim(a, source, 0, False), gathered)
        )

    return lax.fori_loop(0, ahead, one, state)


def pairwise_dot(left_rows, right_rows):
    return lax.dot_general(
        left_rows, right_rows, (((1,), (1,)), ((), ())), preferred_element_type=jnp.float32
    )


def leading_dot(left_rows, right_rows):
    return lax.dot_general(
        left_rows, right_rows, (((0,), (0,)), ((), ())), preferred_element_type=jnp.float32
    )


def combine_states(earlier_item, later_item):
    return (
        jnp.maximum(earlier_item[0], later_item[0]),
        jnp.where(later_item[0] > 0, later_item[1], earlier_item[1] + later_item[1]),
    )


def shards(
    queries,
    key_rows,
    value_rows,
    out_grad,
    cache_states,
    session_start,
    cache_owner,
    probe_gate,
    steer_vector,
):
    length = queries.shape[0]
    heads_here = steer_vector.shape[0]
    scaling = 1.0 / DK
    blocks_total = lax.axis_size("seq")
    block_index = lax.axis_index("seq")
    start_pos = session_start[0]
    reset_flag = (start_pos < length).astype(jnp.float32)
    positions = jnp.arange(length)
    before_start = positions < start_pos
    after_start = positions >= start_pos
    final_part = after_start | (start_pos >= length)
    causal = (positions[None, :] <= positions[:, None]) & (
        after_start[:, None] == after_start[None, :]
    )
    target = cache_owner[block_index]
    zero_state = jnp.zeros((heads_here, DK, DV), jnp.float32)
    shard_piece = lax.all_gather(cache_states, "seq", axis=0, tiled=True)
    slot_ids = jnp.arange(shard_piece.shape[0])
    weights = (slot_ids == target).astype(jnp.bfloat16)
    owned_state = lax.dot_general(
        weights, shard_piece, (((0,), (0,)), ((), ())), preferred_element_type=jnp.float32
    ).astype(jnp.bfloat16)
    query_heads = queries.reshape(length, heads_here, DK)
    key_heads = key_rows.reshape(length, heads_here, DK)
    value_heads = value_rows.reshape(length, heads_here, DV)
    grad_heads = out_grad.reshape(length, heads_here, DV)
    before_mask = before_start.astype(jnp.bfloat16)[:, None]
    after_mask = after_start.astype(jnp.bfloat16)[:, None]
    final_mask = final_part.astype(jnp.bfloat16)[:, None]
    kv_final = jnp.einsum(
        "thd,the->hde",
        key_heads * final_mask[:, :, None],
        value_heads,
        preferred_element_type=jnp.float32,
    )
    tail_state = jnp.where(reset_flag > 0, owned_state.astype(jnp.float32) + kv_final, kv_final)
    head_state = scaling * jnp.einsum(
        "thd,the->hde",
        query_heads * before_mask[:, :, None],
        grad_heads,
        preferred_element_type=jnp.float32,
    )
    start_state = scaling * jnp.einsum(
        "thd,the->hde",
        query_heads * after_mask[:, :, None],
        grad_heads,
        preferred_element_type=jnp.float32,
    )
    identity = (jnp.zeros((), jnp.float32), zero_state)
    entering = prefix((reset_flag, tail_state), "seq", combine_states, identity, False)[1]
    leaving = prefix((reset_flag, head_state), "seq", combine_states, identity, True)[1]
    start_grad = jnp.where(reset_flag > 0, start_state + leaving, 0.0).astype(jnp.bfloat16)
    slot_ids = jnp.arange(lax.axis_size("seq") * 1)
    weights = (slot_ids == target).astype(jnp.float32)
    grad_cache = lax.psum_scatter(
        (weights[:, None, None, None] * start_grad.astype(jnp.float32)[None]).astype(jnp.bfloat16),
        "seq",
        scatter_dimension=0,
        tiled=True,
    )
    entering_low = entering.astype(jnp.bfloat16)
    leaving_low = leaving.astype(jnp.bfloat16)
    query_grads = []
    key_grads = []
    value_grads = []
    for head_index in range(heads_here):
        query_head = queries[:, head_index * DK : (head_index + 1) * DK]
        key_head = key_rows[:, head_index * DK : (head_index + 1) * DK]
        value_head = value_rows[:, head_index * DV : (head_index + 1) * DV]
        grad_head = out_grad[:, head_index * DV : (head_index + 1) * DV]
        grad_scores = jnp.where(causal, scaling * pairwise_dot(grad_head, value_head), 0.0).astype(
            jnp.bfloat16
        )
        key_scores = jnp.where(causal, scaling * pairwise_dot(query_head, key_head), 0.0).astype(
            jnp.bfloat16
        )
        inter_query = pairwise_dot(grad_head * before_mask, entering_low[head_index])
        inter_query = inter_query + pairwise_dot(grad_head * after_mask, owned_state[head_index])
        grad_query = (
            jnp.dot(grad_scores, key_head, preferred_element_type=jnp.float32)
            + scaling * inter_query
        )
        grad_key = leading_dot(grad_scores, query_head) + pairwise_dot(
            value_head * final_mask, leaving_low[head_index]
        )
        grad_value = leading_dot(key_scores, grad_head) + jnp.dot(
            key_head * final_mask, leaving_low[head_index], preferred_element_type=jnp.float32
        )
        query_grads.append(grad_query.astype(jnp.bfloat16))
        key_grads.append(grad_key.astype(jnp.bfloat16))
        value_grads.append(grad_value.astype(jnp.bfloat16))
    grad_queries = jnp.concatenate(query_grads, axis=1)
    grad_keys = jnp.concatenate(key_grads, axis=1)
    grad_values = jnp.concatenate(value_grads, axis=1)
    steer_part = jnp.einsum("t,tc->c", probe_gate, out_grad, preferred_element_type=jnp.float32)
    grad_steer = lax.psum(steer_part, "seq").reshape(heads_here, DV) / math.sqrt(
        length * blocks_total
    )
    gate_part = jnp.dot(out_grad, steer_vector.reshape(-1), preferred_element_type=jnp.float32)
    grad_gate = lax.psum(gate_part, "head")
    return (grad_queries, grad_keys, grad_values, grad_cache, grad_steer, grad_gate)


def solution(mesh):
    in_specs = (
        P("seq", "head"),
        P("seq", "head"),
        P("seq", "head"),
        P("seq", "head"),
        P("seq", "head", None, None),
        P("seq"),
        P(),
        P("seq"),
        P("head", None),
    )
    out_specs = (
        P("seq", "head"),
        P("seq", "head"),
        P("seq", "head"),
        P("seq", "head", None, None),
        P("head", None),
        P("seq"),
    )
    return jax.shard_map(shards, mesh=mesh, in_specs=in_specs, out_specs=out_specs, check_vma=False)
```

profile of v0, /device:TPU:8, one launch (start us, length us, event | category | flops | bytes accessed | tf_op | source)
XLA Modules:
  0.0 521.7 jit_solution(7952977365945046856)
XLA Ops:
  8.6 1.5 copy.37
  10.1 2.8 convolution_multiply_fusion.1
  14.2 81.1 %all-gather.6.cloned.1.call-done = bf16[32,4,128,128]{3,2,1,0:T(8,128)(2,1)} async-done(((bf16[1,4,128,128]{3,2,1,0:T(8,128)(2,1)}), bf16[32,4,128,128]{3,2,1,0:T(8,128)(2,1)}) %all-gather.6.cloned.1.call-update) | async-done | bytes 4194320 | tf_op jit(solution)/shard_map/all_gather | solution.py:73
  95.3 5.4 %fusion = f32[1,4,128,128]{3,0,2,1:T(1,128)S(1)} fusion(bf16[32,4,128,128]{3,2,1,0:T(8,128)(2,1)} %all-gather.6.cloned.1.call-done, s32[]{:T(128)} %bitcast.7), kind=kOutput, calls=%fused_computation.3 | convolution fusion | flops 4194336 | bytes 4456452 | tf_op jit(solution)/shard_map/dot_general | solution.py:76
  100.8 1.1 add_select_fusion.2
  103.7 73.2 %all-reduce.1 = (f32[32]{0:T(128)S(1)}, f32[512]{0:T(512)S(1)}) all-reduce(f32[32]{0:T(128)S(1)} %dynamic-update-slice, f32[512]{0:T(512)S(1)} %bitcast.121), channel_id=1, replica_groups=mesh['seq'=32,'head'=8] {'seq'}, use_global_device_ids=true, to_apply=%add | all-reduce | flops 544 | bytes 4352
  177.2 11.4 %psum.15 = f32[1024]{0:T(1024)} all-reduce(f32[1024]{0:T(1024)S(1)} %bitcast.120), channel_id=1, replica_groups=mesh['seq'=32,'head'=8] {'head'}, use_global_device_ids=true, to_apply=%region_6.7 | all-reduce | flops 1024 | bytes 8192 | tf_op jit(solution)/shard_map/psum | solution.py:156
  189.3 1.8 select_convert_fusion.4
  191.2 1.3 copy-done.6
  192.5 2.2 fusion.66
  195.6 1.3 copy-done.4
  196.9 1.3 fusion.74
  199.0 1.3 copy-done.2
  200.4 1.3 fusion.78
  202.5 72.2 %while.27 = (s32[]{:T(128)}, f32[4,128,128]{2,1,0:T(8,128)S(1)}, s32[]{:T(128)}, f32[32]{0:T(128)S(1)}, f32[32,4,128,128]{3,2,1,0:T(8,128)}, /*index=5*/s32[]{:T(128)}, s32[]{:T(128)}, s32[]{:T(128)}, s32[]{:T(128)}, f32[1]{0:T(128)}) while((s32[]{:T(128)}, f32[4,128,128]{2,1,0:T(8,128)S(1)}, s32[]{:T(128)}, f32[32]{0:T(128)S(1)}, ...), condition=%wide.region_3.4_spmd, body=%wide.region_2.3_spmd.sunk | while | flops 131079 | bytes 786613 | solution.py:24
  203.8 1.1 add_select_fusion.6
  206.1 1.1 add_select_fusion.6
  208.5 1.1 add_select_fusion.6
  210.8 1.1 add_select_fusion.6
  213.1 1.1 add_select_fusion.6
  215.4 1.1 add_select_fusion.6
  217.7 1.1 add_select_fusion.6
  220.1 1.1 add_select_fusion.6
  222.4 1.1 add_select_fusion.6
  224.7 1.1 add_select_fusion.6
  227.0 1.1 add_select_fusion.6
  229.3 1.1 add_select_fusion.6
  231.7 1.1 add_select_fusion.6
  234.0 1.1 add_select_fusion.6
  236.3 1.1 add_select_fusion.6
  238.6 1.1 add_select_fusion.6
  240.9 1.1 add_select_fusion.6
  243.3 1.1 add_select_fusion.6
  245.6 1.1 add_select_fusion.6
  247.9 1.1 add_select_fusion.6
  250.2 1.1 add_select_fusion.6
  252.5 1.1 add_select_fusion.6
  254.9 1.1 add_select_fusion.6
  257.2 1.1 add_select_fusion.6
  259.5 1.1 add_select_fusion.6
  261.8 1.1 add_select_fusion.6
  266.5 1.1 add_select_fusion.6
  268.8 1.1 add_select_fusion.6
  271.1 1.1 add_select_fusion.6
  273.5 1.1 add_select_fusion.6
  274.7 1.7 fusion.26
  276.4 3.1 multiply_convert_fusion
  280.1 2.3 fusion.70
  282.4 3.0 fusion.3
  285.5 3.0 fusion.4
  288.5 3.0 fusion.5
  291.5 3.0 fusion.6
  294.6 1.6 fusion.18
  296.2 1.5 fusion.17
  297.7 1.5 fusion.16
  299.3 1.5 fusion.15
  301.9 2.3 copy.32
  304.1 1.5 fusion.14
  305.7 1.5 fusion.12
  307.2 1.5 fusion.11
  308.7 1.5 fusion.13
  311.3 2.3 copy.31
  320.5 1.3 copy.30
  321.8 193.4 %reduce-scatter.2.cloned.1.call-done = bf16[1,4,128,128]{3,2,1,0:T(8,128)(2,1)} async-done(((bf16[32,4,128,128]{3,2,1,0:T(8,128)(2,1)}), bf16[1,4,128,128]{3,2,1,0:T(8,128)(2,1)}) %reduce-scatter.2.cloned.1.call-update) | async-done | bytes 131088 | tf_op jit(solution)/shard_map/reduce_scatter | solution.py:111
  (116 shorter events, 36.1 us)
Async XLA Ops:
  7.2 96.2 %copy-start = (f32[1024]{0:T(1024)S(1)}, f32[1024]{0:T(1024)}, u32[]{:S(2)}) copy-start(f32[1024]{0:T(1024)} %param.20) | copy-start | bytes 12292
  7.2 5.8 %copy-start.8 = (bf16[1024,512]{1,0:T(8,128)(2,1)S(1)}, bf16[1024,512]{1,0:T(8,128)(2,1)}, u32[]{:S(2)}) copy-start(bf16[1024,512]{1,0:T(8,128)(2,1)} %param.14) | copy-start | bytes 3145732
  7.2 6.4 %copy-start.17 = (s32[32]{0:T(128)S(1)}, s32[32]{0:T(128)}, u32[]{:S(2)}) copy-start(s32[32]{0:T(128)} %param.19) | copy-start | bytes 388
  7.2 88.1 %all-gather.6.cloned.1.call-start = ((), (), s32[]{:S(2)}) async-start(), calls=%async_computation.1 | async-start | bytes 4325376 | tf_op jit(solution)/shard_map/all_gather | solution.py:73
  7.9 194.6 %all-gather.10.cloned.1.call-start = ((), (), s32[]{:S(2)}) async-start(), calls=%async_computation.4 | async-start | bytes 8650752 | tf_op jit(solution)/shard_map/all_gather | solution.py:15
  10.1 85.2 %copy-start.11 = (bf16[1024,512]{0,1:T(8,128)(2,1)}, bf16[1024,512]{0,1:T(8,128)(2,1)S(1)}, u32[]{:S(2)}) copy-start(bf16[1024,512]{0,1:T(8,128)(2,1)S(1)} %copy.37) | copy-start | bytes 3145732
  12.9 300.6 %all-gather.8.cloned.1.call-start = ((), (), s32[]{:S(2)}) async-start(), calls=%async_computation.3 | async-start | bytes 8650752 | tf_op jit(solution)/shard_map/all_gather | solution.py:15
  95.3 5.5 %copy-start.12 = (bf16[1024,512]{1,0:T(8,128)(2,1)S(1)}, bf16[1024,512]{1,0:T(8,128)(2,1)}, u32[]{:S(2)}) copy-start(bf16[1024,512]{1,0:T(8,128)(2,1)} %param.15) | copy-start | bytes 3145732
  95.3 6.7 %copy-start.16 = (bf16[4,128]{1,0:T(4,128)(2,1)S(1)}, bf16[4,128]{1,0:T(4,128)(2,1)}, u32[]{:S(2)}) copy-start(bf16[4,128]{1,0:T(4,128)(2,1)} %param.21) | copy-start | bytes 3076
  95.3 6.7 %copy-start.19 = (u32[256]{0:T(256)S(1)}, u32[256]{0:T(256)}, u32[]{:S(2)}) copy-start(u32[256]{0:T(256)} %constant.87) | copy-start | bytes 3076
  95.3 8.1 %copy-start.1 = (bf16[1024,512]{1,0:T(8,128)(2,1)S(1)}, bf16[1024,512]{1,0:T(8,128)(2,1)}, u32[]{:S(2)}) copy-start(bf16[1024,512]{1,0:T(8,128)(2,1)} %param.16) | copy-start | bytes 3145732
  100.8 88.5 %copy-start.14 = (bf16[4,128,128]{2,1,0:T(8,128)(2,1)}, bf16[4,128,128]{2,1,0:T(8,128)(2,1)S(1)}, u32[]{:S(2)}) copy-start(bf16[4,128,128]{2,1,0:T(8,128)(2,1)S(1)} %convert_element_type.128) | copy-start | bytes 393220
  102.0 413.2 %reduce-scatter.2.cloned.1.call-start = ((), (), s32[]{:S(2)}) async-start(), calls=%async_computation.2 | async-start | bytes 4325376 | tf_op jit(solution)/shard_map/reduce_scatter | solution.py:111
  189.3 5.4 %copy-start.13 = (bf16[1024,512]{1,0:T(8,128)(2,1)S(1)}, bf16[1024,512]{1,0:T(8,128)(2,1)}, u32[]{:S(2)}) copy-start(bf16[1024,512]{1,0:T(8,128)(2,1)} %param.15) | copy-start | bytes 3145732
  191.2 1.3 copy-start.6
  194.8 2.1 copy-start.10
  195.6 1.3 copy-start.4
  199.0 1.4 copy-start.2
  274.7 4.9 copy-start.18
  313.6 1.9 copy-start.15
  313.8 3.2 copy-start.7
  313.9 3.2 copy-start.9
  315.4 2.4 copy-start.5
  316.2 2.5 copy-start.3
Sparse Core Ops, SparseCore 0:
  10.6 84.6 all-gather.5
  98.5 95.9 all-gather.9
  197.0 95.3 all-gather.7
  296.8 218.3 reduce-scatter.1
where the time goes:
time: 524 us; the launch traced here: 522 us
  waiting for transfers between devices  275 us (52%)
  blocking collectives  84.6 us (16%)
  matrix products  53.9 us (10%)
  other arithmetic  39.3 us (7%)
  local copies, waits for them, and re-layouts  32.3 us (6%)
  loops' own time  21.4 us (4%)
  between operations  14.9 us (3%)
    reduce_scatter x1, waiting for transfers between devices, shards(): lax.psum_scatter((weights[:, None, None, None] * start_grad.astype(jnp.fl...  193 us
    all_gather x1, waiting for transfers between devices, shards(): shard_piece = lax.all_gather(cache_states, 'seq', axis=0, tiled=True)  81.1 us
    unnamed x1, blocking collectives  73.2 us
    select_n x31, other arithmetic, combine_states(): jnp.where(later_item[0] > 0, later_item[1], earlier_item[1] + later_item[1])  32.7 us
    another operation x2, loops' own time, prefix(): return lax.fori_loop(0, ahead, one, state)  21.4 us
    dot_general x8, matrix products, leading_dot(): lax.dot_general(left_rows, right_rows, (((0,), (0,)), ((), ())), preferre...  19.3 us
    dynamic_slice x31, local copies, waits for them, and re-layouts, one(): lax.dynamic_index_in_dim(a, source, 0, False)  18.3 us
    dot_general x16, matrix products, pairwise_dot(): lax.dot_general(left_rows, right_rows, (((1,), (1,)), ((), ())), preferre...  13.4 us
  transfers between devices with their start and end apart: 4, of which 2 were waited for; matrix products, arithmetic and copies ran while one was open for 23% of the time, Pallas kernels for 0%

commit v1 on v0

--- a/solution.py
+++ b/solution.py
@@ -70,7 +70,9 @@
     )
     target = cache_owner[block_index]
     zero_state = jnp.zeros((heads_here, DK, DV), jnp.float32)
-    shard_piece = lax.all_gather(cache_states, "seq", axis=0, tiled=True)
+    shard_piece = jnp.concatenate(
+        lax.all_to_all(jnp.stack([cache_states] * lax.axis_size("seq")), "seq", 0, 0), axis=0
+    )
     slot_ids = jnp.arange(shard_piece.shape[0])
     weights = (slot_ids == target).astype(jnp.bfloat16)
     owned_state = lax.dot_general(

time: 524 us -> 560 us (1.069)
  waiting for transfers between devices: 275 us -> 298 us
  starting transfers between devices: 0.16 us -> 11.7 us
    all_to_all x0 -> x1, waiting for transfers between devices: none -> 125 us  [shards(): lax.all_to_all(jnp.stack([cache_states] * lax.axis_size('seq')), 'seq', 0...]
    all_gather x1 -> x0, waiting for transfers between devices: 81.1 us -> none  [shards(): shard_piece = lax.all_gather(cache_states, 'seq', axis=0, tiled=True)]
    reduce_scatter x1, waiting for transfers between devices: 193 us -> 173 us  [shards(): lax.psum_scatter((weights[:, None, None, None] * start_grad.astype(jnp.fl...]
    all_to_all x0 -> x1, starting transfers between devices: none -> 11.6 us  [shards(): lax.all_to_all(jnp.stack([cache_states] * lax.axis_size('seq')), 'seq', 0...]
  transfers between devices with their start and end apart: 4 -> 4, of which waited for: 2 -> 2; matrix products, arithmetic and copies ran while one was open for 23% -> 21% of each run, Pallas kernels for 0% -> 0%
where the time goes in v1:
time: 560 us; the launch traced here: 558 us
  waiting for transfers between devices  298 us (53%)
  blocking collectives  83.9 us (15%)
  matrix products  52.8 us (9%)
  other arithmetic  39.2 us (7%)
  local copies, waits for them, and re-layouts  35.9 us (6%)
  loops' own time  21.4 us (4%)
  between operations  14.9 us (3%)
  starting transfers between devices  11.7 us (2%)
    reduce_scatter x1, waiting for transfers between devices, shards(): lax.psum_scatter((weights[:, None, None, None] * start_grad.astype(jnp.fl...  173 us
    all_to_all x1, waiting for transfers between devices, shards(): lax.all_to_all(jnp.stack([cache_states] * lax.axis_size('seq')), 'seq', 0...  125 us
    unnamed x1, blocking collectives  72.5 us
    select_n x31, other arithmetic, combine_states(): jnp.where(later_item[0] > 0, later_item[1], earlier_item[1] + later_item[1])  32.7 us
    another operation x2, loops' own time, prefix(): return lax.fori_loop(0, ahead, one, state)  21.4 us
    dot_general x8, matrix products, leading_dot(): lax.dot_general(left_rows, right_rows, (((0,), (0,)), ((), ())), preferre...  18.3 us
    dynamic_slice x31, local copies, waits for them, and re-layouts, one(): lax.dynamic_index_in_dim(a, source, 0, False)  18.3 us
    dot_general x16, matrix products, pairwise_dot(): lax.dot_general(left_rows, right_rows, (((1,), (1,)), ((), ())), preferre...  13.3 us
  transfers between devices with their start and end apart: 4, of which 2 were waited for; matrix products, arithmetic and copies ran while one was open for 21% of the time, Pallas kernels for 0%

profile of v1, /device:TPU:8, one launch (start us, length us, event | category | flops | bytes accessed | tf_op | source)
XLA Modules:
  0.0 558.0 jit_solution(3068177628957482658)
XLA Ops:
  7.9 1.5 copy.37
  9.4 2.8 convolution_multiply_fusion.1
  12.2 3.1 stack.2
  15.3 11.6 %all-to-all-start = ((bf16[32,1,4,128,128]{4,3,2,1,0:T(8,128)(2,1)}), bf16[32,1,4,128,128]{4,3,2,1,0:T(8,128)(2,1)}, u32[]{:S(2)}, u32[]{:S(2)}) async-start(bf16[32,1,4,128,128]{4,3,2,1,0:T(8,128)(2,1)} %stack.2), calls=%async_computation | async-start | bytes 8388608 | tf_op jit(solution)/shard_map/all_to_all | solution.py:74
  28.1 125.1 %all-to-all-done = bf16[32,1,4,128,128]{4,3,2,1,0:T(8,128)(2,1)} async-done(((bf16[32,1,4,128,128]{4,3,2,1,0:T(8,128)(2,1)}), bf16[32,1,4,128,128]{4,3,2,1,0:T(8,128)(2,1)}, u32[]{:S(2)}, u32[]{:S(2)}) %all-to-all-start) | async-done | bytes 4194336 | tf_op jit(solution)/shard_map/all_to_all | solution.py:74
  153.2 5.4 fusion
  159.3 1.2 add_select_fusion.2
  162.2 72.5 %all-reduce.1 = (f32[32]{0:T(128)S(1)}, f32[512]{0:T(512)S(1)}) all-reduce(f32[32]{0:T(128)S(1)} %dynamic-update-slice, f32[512]{0:T(512)S(1)} %bitcast.124), channel_id=1, replica_groups=mesh['seq'=32,'head'=8] {'seq'}, use_global_device_ids=true, to_apply=%add | all-reduce | flops 544 | bytes 4352
  235.1 11.4 %psum.15 = f32[1024]{0:T(1024)} all-reduce(f32[1024]{0:T(1024)S(1)} %bitcast.123), channel_id=1, replica_groups=mesh['seq'=32,'head'=8] {'head'}, use_global_device_ids=true, to_apply=%region_6.7 | all-reduce | flops 1024 | bytes 8192 | tf_op jit(solution)/shard_map/psum | solution.py:158
  248.0 1.3 copy-done.6
  249.3 1.3 fusion.66
  251.4 1.3 copy-done.4
  252.7 1.3 fusion.70
  254.8 1.4 copy-done.2
  256.2 1.3 fusion.74
  257.5 1.8 select_convert_fusion.7
  259.3 72.0 %while.27 = (s32[]{:T(128)}, f32[4,128,128]{2,1,0:T(8,128)S(1)}, s32[]{:T(128)}, f32[32]{0:T(128)S(1)}, f32[32,4,128,128]{3,2,1,0:T(8,128)}, /*index=5*/s32[]{:T(128)}, s32[]{:T(128)}, s32[]{:T(128)}, s32[]{:T(128)}, f32[1]{0:T(128)}) while((s32[]{:T(128)}, f32[4,128,128]{2,1,0:T(8,128)S(1)}, s32[]{:T(128)}, f32[32]{0:T(128)S(1)}, ...), condition=%wide.region_3.4_spmd, body=%wide.region_2.3_spmd.sunk | while | flops 131079 | bytes 786613 | solution.py:24
  260.6 1.1 add_select_fusion.6
  262.9 1.1 add_select_fusion.6
  265.2 1.1 add_select_fusion.6
  267.5 1.1 add_select_fusion.6
  269.8 1.1 add_select_fusion.6
  272.2 1.1 add_select_fusion.6
  274.5 1.1 add_select_fusion.6
  276.8 1.1 add_select_fusion.6
  279.1 1.1 add_select_fusion.6
  283.8 1.1 add_select_fusion.6
  286.1 1.1 add_select_fusion.6
  288.4 1.1 add_select_fusion.6
  290.7 1.1 add_select_fusion.6
  293.0 1.1 add_select_fusion.6
  295.3 1.1 add_select_fusion.6
  297.7 1.1 add_select_fusion.6
  300.0 1.1 add_select_fusion.6
  302.3 1.1 add_select_fusion.6
  304.6 1.1 add_select_fusion.6
  306.9 1.1 add_select_fusion.6
  309.3 1.1 add_select_fusion.6
  311.6 1.1 add_select_fusion.6
  313.9 1.1 add_select_fusion.6
  318.5 1.1 add_select_fusion.6
  320.8 1.1 add_select_fusion.6
  323.2 1.1 add_select_fusion.6
  327.8 1.1 add_select_fusion.6
  330.1 1.1 add_select_fusion.6
  331.4 1.7 fusion.26
  333.1 3.1 multiply_convert_fusion
  336.8 2.2 fusion.78
  339.0 3.1 fusion.6
  342.1 3.0 fusion.5
  345.2 3.0 fusion.4
  348.2 3.0 fusion.3
  351.3 1.5 fusion.14
  352.8 1.5 fusion.13
  354.3 1.5 fusion.12
  355.8 1.5 fusion.11
  358.4 2.3 copy.31
  360.7 1.5 fusion.18
  362.2 1.6 fusion.17
  363.8 1.6 fusion.16
  365.4 1.6 fusion.15
  368.0 2.3 copy.32
  377.1 1.3 copy.30
  378.5 173.0 %reduce-scatter.2.cloned.1.call-done = bf16[1,4,128,128]{3,2,1,0:T(8,128)(2,1)} async-done(((bf16[32,4,128,128]{3,2,1,0:T(8,128)(2,1)}), bf16[1,4,128,128]{3,2,1,0:T(8,128)(2,1)}) %reduce-scatter.2.cloned.1.call-update) | async-done | bytes 131088 | tf_op jit(solution)/shard_map/reduce_scatter | solution.py:113
  (116 shorter events, 38.0 us)
Async XLA Ops:
  7.2 154.7 %copy-start = (f32[1024]{0:T(1024)S(1)}, f32[1024]{0:T(1024)}, u32[]{:S(2)}) copy-start(f32[1024]{0:T(1024)} %param.20) | copy-start | bytes 12292
  7.2 5.0 copy-start.15
  7.2 252.1 %all-gather.7.cloned.1.call-start = ((), (), s32[]{:S(2)}) async-start(), calls=%async_computation.4 | async-start | bytes 8650752 | tf_op jit(solution)/shard_map/all_gather | solution.py:15
  9.4 2.8 copy-start.11
  15.3 11.7 %copy-start.8 = (bf16[1024,512]{1,0:T(8,128)(2,1)S(1)}, bf16[1024,512]{1,0:T(8,128)(2,1)}, u32[]{:S(2)}) copy-start(bf16[1024,512]{1,0:T(8,128)(2,1)} %param.14) | copy-start | bytes 3145732
  15.3 12.2 %copy-start.17 = (s32[32]{0:T(128)S(1)}, s32[32]{0:T(128)}, u32[]{:S(2)}) copy-start(s32[32]{0:T(128)} %param.19) | copy-start | bytes 388
  15.3 137.9 %all-to-all-start = ((bf16[32,1,4,128,128]{4,3,2,1,0:T(8,128)(2,1)}), bf16[32,1,4,128,128]{4,3,2,1,0:T(8,128)(2,1)}, u32[]{:S(2)}, u32[]{:S(2)}) async-start(bf16[32,1,4,128,128]{4,3,2,1,0:T(8,128)(2,1)} %stack.2), calls=%async_computation | async-start | bytes 8388608 | tf_op jit(solution)/shard_map/all_to_all | solution.py:74
  26.9 132.4 %copy-start.12 = (bf16[1024,512]{1,0:T(8,128)(2,1)S(1)}, bf16[1024,512]{1,0:T(8,128)(2,1)}, u32[]{:S(2)}) copy-start(bf16[1024,512]{1,0:T(8,128)(2,1)} %param.15) | copy-start | bytes 3145732
  26.9 343.3 %all-gather.5.cloned.1.call-start = ((), (), s32[]{:S(2)}) async-start(), calls=%async_computation.3 | async-start | bytes 8650752 | tf_op jit(solution)/shard_map/all_gather | solution.py:15
  153.2 7.3 %copy-start.16 = (bf16[4,128]{1,0:T(4,128)(2,1)S(1)}, bf16[4,128]{1,0:T(4,128)(2,1)}, u32[]{:S(2)}) copy-start(bf16[4,128]{1,0:T(4,128)(2,1)} %param.21) | copy-start | bytes 3076
  153.2 7.3 %copy-start.19 = (u32[256]{0:T(256)S(1)}, u32[256]{0:T(256)}, u32[]{:S(2)}) copy-start(u32[256]{0:T(256)} %constant.87) | copy-start | bytes 3076
  153.2 8.7 %copy-start.1 = (bf16[1024,512]{1,0:T(8,128)(2,1)S(1)}, bf16[1024,512]{1,0:T(8,128)(2,1)}, u32[]{:S(2)}) copy-start(bf16[1024,512]{1,0:T(8,128)(2,1)} %param.16) | copy-start | bytes 3145732
  158.6 0.7 copy-start.13
  160.5 391.0 %reduce-scatter.2.cloned.1.call-start = ((), (), s32[]{:S(2)}) async-start(), calls=%async_computation.2 | async-start | bytes 4325376 | tf_op jit(solution)/shard_map/reduce_scatter | solution.py:113
  162.2 87.1 %copy-start.10 = (bf16[1024,512]{1,0:T(8,128)(2,1)S(1)}, bf16[1024,512]{1,0:T(8,128)(2,1)}, u32[]{:S(2)}) copy-start(bf16[1024,512]{1,0:T(8,128)(2,1)} %param.13) | copy-start | bytes 3145732
  247.9 1.3 copy-start.6
  251.4 1.3 copy-start.4
  254.8 1.4 copy-start.2
  331.4 4.8 copy-start.18
  370.2 1.9 copy-start.14
  370.5 3.2 copy-start.7
  370.5 3.2 copy-start.9
  372.1 2.4 copy-start.5
  372.9 2.5 copy-start.3
Sparse Core Ops, SparseCore 0:
  12.3 157.5 all-gather.6
  172.5 97.2 all-gather.4
  336.3 215.1 reduce-scatter.1
